TPU v7x, 128 devices: a whole 4x4x4 slice. The times are simulated.
128 devices in a mesh: tensor: 8 (over y_hi, x), context: 16 (over z, y_lo, core).
Axes of the slice: x: 4, y: 4 (y_hi: 2, y_lo: 2; y = y_hi * 2 + y_lo), z: 4, core: 2. Of those that a mesh axis runs over, the one named last changes fastest.
Arguments:
- tokens: bfloat16 [16, 1024, 4096], P('context', 'tensor'), may hold values from -6 to 6
- norm_gain: float32 [4096], replicated, may hold values from 0.25 to 1.75
- q_weight: bfloat16 [4096, 2048], P(None, 'tensor')
- k_weight: bfloat16 [4096, 1024], P(None, 'tensor')
- v_weight: bfloat16 [4096, 1024], P(None, 'tensor'), may hold values from -0.75 to 0.75
- o_weight: bfloat16 [2048, 4096], P('tensor'), may hold values from -0.125 to 0.125
- doc_lengths: int32 [16], replicated, may hold values from 1 to 4096, 16384 in all
- span_order: int32 [32], replicated, may hold values from 0 to 31, each once
Outputs:
- layer_out: bfloat16 [16, 1024, 4096], P('context', 'tensor')
Inputs may be any that keep to these rules, and one draw needn't show every extreme that they name: `doc_lengths`: documents fill the sequence in order; the longest has exactly 4096 tokens. `span_order`: each value appears once.
All inputs are finite; a program needn't handle non-finite values.
Results may differ from a plain program's by a relative error of at most 0.019.
Values may be sent and summed in bfloat16 or wider, within the bound.
A program may use at most 320 MiB of HBM per device.

v0:
```python
import math
import jax
import jax.numpy as jnp
from jax import lax
from jax.sharding import PartitionSpec as P

HEAD_DIM = 128
rope_theta = 500000.0
epsilon = 1e-05
masked_score = -1e30


def positions(rows, span_order, span_rows):
    slot_ids = jnp.arange(span_order.shape[0], dtype=jnp.int32)
    matches = (rows // span_rows)[:, None] == slot_ids[None, :]
    picked = jnp.sum(jnp.where(matches, span_order[None, :], 0), axis=1)
    return picked * span_rows + rows % span_rows


def documents(places, doc_lengths):
    doc_ends = jnp.cumsum(doc_lengths)
    return jnp.sum((doc_ends[None, :] <= places[:, None]).astype(jnp.int32), axis=1)


def rotary(values, places):
    head_dim = values.shape[-1]
    half_dim = head_dim // 2
    frequency = rope_theta ** (-(2.0 / head_dim) * jnp.arange(half_dim, dtype=jnp.float32))
    angles = places.astype(jnp.float32)[:, None] * frequency[None, :]
    cosine = jnp.cos(angles)[:, None, :]
    sine_part = jnp.sin(angles)[:, None, :]
    first_half = values[..., :half_dim]
    second = values[..., half_dim:]
    return jnp.concatenate(
        [first_half * cosine - second * sine_part, second * cosine + first_half * sine_part],
        axis=-1,
    )


def per_device(tokens, norm_gain, q_weight, k_weight, v_weight, o_weight, doc_lengths, span_order):
    local_rows = tokens.shape[1]
    tok_dev = local_rows * lax.axis_size("tensor")
    model_width = tokens.shape[2]
    head_dim = HEAD_DIM
    q_cols = q_weight.shape[1]
    kv_cols = k_weight.shape[1]
    q_heads = q_cols // head_dim
    kv_local = kv_cols // head_dim
    group_size = q_heads // kv_local
    span_rows = tok_dev // 2
    base_row = lax.axis_index("context") * tok_dev
    score_scale = 1.0 / math.sqrt(head_dim)
    rows_float = tokens.astype(jnp.float32)
    normed = (
        rows_float
        * lax.rsqrt(jnp.mean(rows_float * rows_float, axis=-1, keepdims=True) + epsilon)
        * norm_gain
    ).astype(jnp.bfloat16)
    portion = lax.all_gather(normed, "tensor", axis=1, tiled=True)
    row_count = portion.shape[1]
    flat_rows = portion.reshape(row_count, model_width)
    places = positions(base_row + jnp.arange(row_count, dtype=jnp.int32), span_order, span_rows)
    query_rows = jnp.dot(flat_rows, q_weight, preferred_element_type=jnp.float32).reshape(
        row_count, q_heads, head_dim
    )
    key_rows = jnp.dot(flat_rows, k_weight, preferred_element_type=jnp.float32).reshape(
        row_count, kv_local, head_dim
    )
    value_rows = jnp.dot(flat_rows, v_weight, preferred_element_type=jnp.float32).astype(
        jnp.bfloat16
    )
    query_rows = rotary(query_rows, places).reshape(row_count, q_cols).astype(jnp.bfloat16)
    key_rows = rotary(key_rows, places).reshape(row_count, kv_cols).astype(jnp.bfloat16)
    projected = jnp.concatenate([query_rows, key_rows, value_rows], axis=1)[None][0]
    query_places = positions(base_row + jnp.arange(tok_dev, dtype=jnp.int32), span_order, span_rows)
    query_docs = documents(query_places, doc_lengths)
    queries = projected[:, :q_cols].reshape(tok_dev, kv_local, group_size, head_dim)
    kv_pair = jnp.stack([projected[:, q_cols : q_cols + kv_cols], projected[:, q_cols + kv_cols :]])

    def attend(running, portion, offset):
        row_count = portion.shape[1]
        key_places = positions(
            offset + jnp.arange(row_count, dtype=jnp.int32), span_order, span_rows
        )
        key_docs = documents(key_places, doc_lengths)
        visible = (key_places[None, :] <= query_places[:, None]) & (
            key_docs[None, :] == query_docs[:, None]
        )
        running_max, row_sum, weighted = running
        key_rows = portion[0].reshape(row_count, kv_local, head_dim)
        value_rows = portion[1].reshape(row_count, kv_local, head_dim)
        scores = (
            jnp.einsum("qkgd,skd->kgqs", queries, key_rows, preferred_element_type=jnp.float32)
            * score_scale
        )
        limited = jnp.where(visible, scores, masked_score)
        new_max = jnp.maximum(running_max, jnp.max(limited, axis=-1))
        factor = jnp.exp(running_max - new_max)
        weights = jnp.where(visible, jnp.exp(scores - new_max[..., None]), 0.0)
        row_sum = row_sum * factor + jnp.sum(weights, axis=-1)
        weighted = weighted * factor.transpose(2, 0, 1)[..., None] + jnp.einsum(
            "kgqs,skd->qkgd",
            weights.astype(jnp.bfloat16),
            value_rows,
            preferred_element_type=jnp.float32,
        )
        return (new_max, row_sum, weighted)

    initial = (
        jnp.full((kv_local, group_size, tok_dev), masked_score, jnp.float32),
        jnp.zeros((kv_local, group_size, tok_dev), jnp.float32),
        jnp.zeros((tok_dev, kv_local, group_size, head_dim), jnp.float32),
    )
    gathered = lax.all_gather(kv_pair, "context", axis=1, tiled=True)

    def visit_block(block_index, carried):
        offset = block_index * tok_dev
        portion = lax.dynamic_slice_in_dim(gathered, offset, tok_dev, 1)
        return attend(carried, portion, offset)

    running_max, row_sum, weighted = lax.fori_loop(
        0, lax.axis_size("context"), visit_block, initial
    )
    attended = (
        (weighted / row_sum.transpose(2, 0, 1)[..., None])
        .reshape(tok_dev, q_cols)
        .astype(jnp.bfloat16)
    )
    mixed_rows = lax.psum_scatter(
        jnp.dot(attended, o_weight, preferred_element_type=jnp.float32).astype(jnp.bfloat16),
        "tensor",
        scatter_dimension=0,
        tiled=True,
    )
    return mixed_rows.reshape(tokens.shape)


def solution(mesh):
    in_specs = (
        P("context", "tensor", None),
        P(),
        P(None, "tensor"),
        P(None, "tensor"),
        P(None, "tensor"),
        P("tensor", None),
        P(),
        P(),
    )
    out_specs = P("context", "tensor", None)
    return jax.shard_map(
        per_device, mesh=mesh, in_specs=in_specs, out_specs=out_specs, check_vma=False
    )
```

profile of v0, /device:TPU:1, one launch (start us, length us, event | category | flops | bytes accessed | tf_op | source)
XLA Modules:
  0.0 585.3 jit_solution(13166002887668406212)
XLA Ops:
  8.2 2.5 fusion.36
  11.7 110.9 %all-gather.3.cloned.1.call-done = bf16[1,1024,4096]{2,1,0:T(8,128)(2,1)} async-done(((bf16[1,128,4096]{2,1,0:T(8,128)(2,1)}), bf16[1,1024,4096]{2,1,0:T(8,128)(2,1)}) %all-gather.3.cloned.1.call-update) | async-done | bytes 8388624 | tf_op jit(solution)/shard_map/all_gather | solution.py:59
  122.6 6.7 %fusion.37 = f32[1024,1,128]{0,2,1:T(8,128)S(1)} fusion(bf16[4096,128]{1,0:T(8,128)(2,1)} %param.13, bf16[1,1024,4096]{2,1,0:T(8,128)(2,1)} %all-gather.3.cloned.1.call-done), kind=kOutput, calls=%fused_computation.56 | convolution fusion | flops 1073741824 | bytes 9961472 | tf_op jit(solution)/shard_map/dot_general | solution.py:66
  130.5 2.9 fusion.43
  134.5 4.1 copy.24
  139.9 6.7 %fusion.28 = f32[1024,2,128]{0,2,1:T(8,128)S(1)} fusion(bf16[2,128,4096]{2,1,0:T(8,128)(2,1)} %bitcast.129, bf16[1,1024,4096]{2,1,0:T(8,128)(2,1)} %all-gather.3.cloned.1.call-done), kind=kOutput, calls=%fused_computation.44 | convolution fusion | flops 2147483648 | bytes 11534336 | tf_op jit(solution)/shard_map/dot_general | solution.py:63
  147.8 37.5 %all-gather.5.cloned.1.call-done = bf16[2,16384,128]{1,2,0:T(8,128)(2,1)} async-done(((bf16[2,1024,128]{1,2,0:T(8,128)(2,1)}), bf16[2,16384,128]{1,2,0:T(8,128)(2,1)}) %all-gather.5.cloned.1.call-update) | async-done | bytes 8388624 | tf_op jit(solution)/shard_map/all_gather | solution.py:114
  185.3 270.9 %while.20 = (s32[]{:T(128)}, f32[1,2,1024]{2,1,0:T(2,128)S(1)}, f32[1,2,1024]{2,1,0:T(2,128)S(1)}, f32[1024,1,2,128]{0,3,2,1:T(8,128)}, s32[32]{0:T(128)S(1)}, /...) while((s32[]{:T(128)}, f32[1,2,1024]{2,1,0:T(2,128)S(1)}, ...), condition=%wide.region_9.10_spmd.clone, body=%wide.region_4.9_spmd.clone.sunk | while | flops 1100931072 | bytes 66236864 | solution.py:121
  186.7 6.3 %fusion.77 = (f32[2,1024]{1,0:T(2,128)S(1)}, f32[1024,1024,2]{1,0,2:T(8,128)}) fusion(pred[1024,1024]{0,1:T(8,128)(4,1)S(1)} %compare_and_fusion.2, bf16[1024,1,2,128]{3,0,2,1:T(8,128)(2,1)} %get-tuple-element.448, bf16[2,16384,128]{1,2,0:T(8,128)(2,1)} %get-tuple-element.447, s32[]{:T(128)S(6)} %select_n.164), kind=kOutput, calls=%fused_computation.2.clone.1 | convolution fusion | flops 543160320 | bytes 10231812 | tf_op jit(solution)/shard_map/while/body/eval_jaxpr/qkgd,skd->kgqs/dot_general | solution.py:93
  193.0 7.0 %fusion.80 = f32[1024,1,2,128]{0,3,2,1:T(8,128)} fusion(f32[1024,1024,2]{1,0,2:T(8,128)} %get-tuple-element.407, f32[2,1024]{1,0:T(2,128)S(1)} %bitcast.126, pred[1024,1024]{0,1:T(8,128)(4,1)S(1)} %compare_and_fusion.2, f32[1024,1,2,128]{0,3,2,1:T(8,128)} %get-tuple-element.427, f32[1024,2]{0,1:T(2,128)S(1)} %get-tuple-element.408, ...), kind=kOutput, calls=%fused_computation.12.clone.1 | convolution fusion | flops 546045952 | bytes 11812873 | tf_op jit(solution)/shard_map/while/body/eval_jaxpr/kgqs,skd->qkgd/dot_general | solution.py:101
  200.0 2.0 fusion.79
  203.5 6.3 %fusion.77 = (f32[2,1024]{1,0:T(2,128)S(1)}, f32[1024,1024,2]{1,0,2:T(8,128)}) fusion(pred[1024,1024]{0,1:T(8,128)(4,1)S(1)} %compare_and_fusion.2, bf16[1024,1,2,128]{3,0,2,1:T(8,128)(2,1)} %get-tuple-element.448, bf16[2,16384,128]{1,2,0:T(8,128)(2,1)} %get-tuple-element.447, s32[]{:T(128)S(6)} %select_n.164), kind=kOutput, calls=%fused_computation.2.clone.1 | convolution fusion | flops 543160320 | bytes 10231812 | tf_op jit(solution)/shard_map/while/body/eval_jaxpr/qkgd,skd->kgqs/dot_general | solution.py:93
  209.8 7.2 %fusion.80 = f32[1024,1,2,128]{0,3,2,1:T(8,128)} fusion(f32[1024,1024,2]{1,0,2:T(8,128)} %get-tuple-element.407, f32[2,1024]{1,0:T(2,128)S(1)} %bitcast.126, pred[1024,1024]{0,1:T(8,128)(4,1)S(1)} %compare_and_fusion.2, f32[1024,1,2,128]{0,3,2,1:T(8,128)} %get-tuple-element.427, f32[1024,2]{0,1:T(2,128)S(1)} %get-tuple-element.408, ...), kind=kOutput, calls=%fused_computation.12.clone.1 | convolution fusion | flops 546045952 | bytes 11812873 | tf_op jit(solution)/shard_map/while/body/eval_jaxpr/kgqs,skd->qkgd/dot_general | solution.py:101
  217.0 2.0 fusion.79
  220.4 6.3 %fusion.77 = (f32[2,1024]{1,0:T(2,128)S(1)}, f32[1024,1024,2]{1,0,2:T(8,128)}) fusion(pred[1024,1024]{0,1:T(8,128)(4,1)S(1)} %compare_and_fusion.2, bf16[1024,1,2,128]{3,0,2,1:T(8,128)(2,1)} %get-tuple-element.448, bf16[2,16384,128]{1,2,0:T(8,128)(2,1)} %get-tuple-element.447, s32[]{:T(128)S(6)} %select_n.164), kind=kOutput, calls=%fused_computation.2.clone.1 | convolution fusion | flops 543160320 | bytes 10231812 | tf_op jit(solution)/shard_map/while/body/eval_jaxpr/qkgd,skd->kgqs/dot_general | solution.py:93
  226.7 7.2 %fusion.80 = f32[1024,1,2,128]{0,3,2,1:T(8,128)} fusion(f32[1024,1024,2]{1,0,2:T(8,128)} %get-tuple-element.407, f32[2,1024]{1,0:T(2,128)S(1)} %bitcast.126, pred[1024,1024]{0,1:T(8,128)(4,1)S(1)} %compare_and_fusion.2, f32[1024,1,2,128]{0,3,2,1:T(8,128)} %get-tuple-element.427, f32[1024,2]{0,1:T(2,128)S(1)} %get-tuple-element.408, ...), kind=kOutput, calls=%fused_computation.12.clone.1 | convolution fusion | flops 546045952 | bytes 11812873 | tf_op jit(solution)/shard_map/while/body/eval_jaxpr/kgqs,skd->qkgd/dot_general | solution.py:101
  237.4 6.3 %fusion.77 = (f32[2,1024]{1,0:T(2,128)S(1)}, f32[1024,1024,2]{1,0,2:T(8,128)}) fusion(pred[1024,1024]{0,1:T(8,128)(4,1)S(1)} %compare_and_fusion.2, bf16[1024,1,2,128]{3,0,2,1:T(8,128)(2,1)} %get-tuple-element.448, bf16[2,16384,128]{1,2,0:T(8,128)(2,1)} %get-tuple-element.447, s32[]{:T(128)S(6)} %select_n.164), kind=kOutput, calls=%fused_computation.2.clone.1 | convolution fusion | flops 543160320 | bytes 10231812 | tf_op jit(solution)/shard_map/while/body/eval_jaxpr/qkgd,skd->kgqs/dot_general | solution.py:93
  243.7 7.2 %fusion.80 = f32[1024,1,2,128]{0,3,2,1:T(8,128)} fusion(f32[1024,1024,2]{1,0,2:T(8,128)} %get-tuple-element.407, f32[2,1024]{1,0:T(2,128)S(1)} %bitcast.126, pred[1024,1024]{0,1:T(8,128)(4,1)S(1)} %compare_and_fusion.2, f32[1024,1,2,128]{0,3,2,1:T(8,128)} %get-tuple-element.427, f32[1024,2]{0,1:T(2,128)S(1)} %get-tuple-element.408, ...), kind=kOutput, calls=%fused_computation.12.clone.1 | convolution fusion | flops 546045952 | bytes 11812873 | tf_op jit(solution)/shard_map/while/body/eval_jaxpr/kgqs,skd->qkgd/dot_general | solution.py:101
  250.9 2.0 fusion.79
  254.3 6.3 %fusion.77 = (f32[2,1024]{1,0:T(2,128)S(1)}, f32[1024,1024,2]{1,0,2:T(8,128)}) fusion(pred[1024,1024]{0,1:T(8,128)(4,1)S(1)} %compare_and_fusion.2, bf16[1024,1,2,128]{3,0,2,1:T(8,128)(2,1)} %get-tuple-element.448, bf16[2,16384,128]{1,2,0:T(8,128)(2,1)} %get-tuple-element.447, s32[]{:T(128)S(6)} %select_n.164), kind=kOutput, calls=%fused_computation.2.clone.1 | convolution fusion | flops 543160320 | bytes 10231812 | tf_op jit(solution)/shard_map/while/body/eval_jaxpr/qkgd,skd->kgqs/dot_general | solution.py:93
  260.6 7.2 %fusion.80 = f32[1024,1,2,128]{0,3,2,1:T(8,128)} fusion(f32[1024,1024,2]{1,0,2:T(8,128)} %get-tuple-element.407, f32[2,1024]{1,0:T(2,128)S(1)} %bitcast.126, pred[1024,1024]{0,1:T(8,128)(4,1)S(1)} %compare_and_fusion.2, f32[1024,1,2,128]{0,3,2,1:T(8,128)} %get-tuple-element.427, f32[1024,2]{0,1:T(2,128)S(1)} %get-tuple-element.408, ...), kind=kOutput, calls=%fused_computation.12.clone.1 | convolution fusion | flops 546045952 | bytes 11812873 | tf_op jit(solution)/shard_map/while/body/eval_jaxpr/kgqs,skd->qkgd/dot_general | solution.py:101
  267.8 2.0 fusion.79
  271.2 6.3 %fusion.77 = (f32[2,1024]{1,0:T(2,128)S(1)}, f32[1024,1024,2]{1,0,2:T(8,128)}) fusion(pred[1024,1024]{0,1:T(8,128)(4,1)S(1)} %compare_and_fusion.2, bf16[1024,1,2,128]{3,0,2,1:T(8,128)(2,1)} %get-tuple-element.448, bf16[2,16384,128]{1,2,0:T(8,128)(2,1)} %get-tuple-element.447, s32[]{:T(128)S(6)} %select_n.164), kind=kOutput, calls=%fused_computation.2.clone.1 | convolution fusion | flops 543160320 | bytes 10231812 | tf_op jit(solution)/shard_map/while/body/eval_jaxpr/qkgd,skd->kgqs/dot_general | solution.py:93
  277.5 7.2 %fusion.80 = f32[1024,1,2,128]{0,3,2,1:T(8,128)} fusion(f32[1024,1024,2]{1,0,2:T(8,128)} %get-tuple-element.407, f32[2,1024]{1,0:T(2,128)S(1)} %bitcast.126, pred[1024,1024]{0,1:T(8,128)(4,1)S(1)} %compare_and_fusion.2, f32[1024,1,2,128]{0,3,2,1:T(8,128)} %get-tuple-element.427, f32[1024,2]{0,1:T(2,128)S(1)} %get-tuple-element.408, ...), kind=kOutput, calls=%fused_computation.12.clone.1 | convolution fusion | flops 546045952 | bytes 11812873 | tf_op jit(solution)/shard_map/while/body/eval_jaxpr/kgqs,skd->qkgd/dot_general | solution.py:101
  284.7 2.0 fusion.79
  288.2 6.3 %fusion.77 = (f32[2,1024]{1,0:T(2,128)S(1)}, f32[1024,1024,2]{1,0,2:T(8,128)}) fusion(pred[1024,1024]{0,1:T(8,128)(4,1)S(1)} %compare_and_fusion.2, bf16[1024,1,2,128]{3,0,2,1:T(8,128)(2,1)} %get-tuple-element.448, bf16[2,16384,128]{1,2,0:T(8,128)(2,1)} %get-tuple-element.447, s32[]{:T(128)S(6)} %select_n.164), kind=kOutput, calls=%fused_computation.2.clone.1 | convolution fusion | flops 543160320 | bytes 10231812 | tf_op jit(solution)/shard_map/while/body/eval_jaxpr/qkgd,skd->kgqs/dot_general | solution.py:93
  294.5 7.2 %fusion.80 = f32[1024,1,2,128]{0,3,2,1:T(8,128)} fusion(f32[1024,1024,2]{1,0,2:T(8,128)} %get-tuple-element.407, f32[2,1024]{1,0:T(2,128)S(1)} %bitcast.126, pred[1024,1024]{0,1:T(8,128)(4,1)S(1)} %compare_and_fusion.2, f32[1024,1,2,128]{0,3,2,1:T(8,128)} %get-tuple-element.427, f32[1024,2]{0,1:T(2,128)S(1)} %get-tuple-element.408, ...), kind=kOutput, calls=%fused_computation.12.clone.1 | convolution fusion | flops 546045952 | bytes 11812873 | tf_op jit(solution)/shard_map/while/body/eval_jaxpr/kgqs,skd->qkgd/dot_general | solution.py:101
  301.7 2.0 fusion.79
  305.1 6.3 %fusion.77 = (f32[2,1024]{1,0:T(2,128)S(1)}, f32[1024,1024,2]{1,0,2:T(8,128)}) fusion(pred[1024,1024]{0,1:T(8,128)(4,1)S(1)} %compare_and_fusion.2, bf16[1024,1,2,128]{3,0,2,1:T(8,128)(2,1)} %get-tuple-element.448, bf16[2,16384,128]{1,2,0:T(8,128)(2,1)} %get-tuple-element.447, s32[]{:T(128)S(6)} %select_n.164), kind=kOutput, calls=%fused_computation.2.clone.1 | convolution fusion | flops 543160320 | bytes 10231812 | tf_op jit(solution)/shard_map/while/body/eval_jaxpr/qkgd,skd->kgqs/dot_general | solution.py:93
  311.4 7.2 %fusion.80 = f32[1024,1,2,128]{0,3,2,1:T(8,128)} fusion(f32[1024,1024,2]{1,0,2:T(8,128)} %get-tuple-element.407, f32[2,1024]{1,0:T(2,128)S(1)} %bitcast.126, pred[1024,1024]{0,1:T(8,128)(4,1)S(1)} %compare_and_fusion.2, f32[1024,1,2,128]{0,3,2,1:T(8,128)} %get-tuple-element.427, f32[1024,2]{0,1:T(2,128)S(1)} %get-tuple-element.408, ...), kind=kOutput, calls=%fused_computation.12.clone.1 | convolution fusion | flops 546045952 | bytes 11812873 | tf_op jit(solution)/shard_map/while/body/eval_jaxpr/kgqs,skd->qkgd/dot_general | solution.py:101
  322.1 6.3 %fusion.77 = (f32[2,1024]{1,0:T(2,128)S(1)}, f32[1024,1024,2]{1,0,2:T(8,128)}) fusion(pred[1024,1024]{0,1:T(8,128)(4,1)S(1)} %compare_and_fusion.2, bf16[1024,1,2,128]{3,0,2,1:T(8,128)(2,1)} %get-tuple-element.448, bf16[2,16384,128]{1,2,0:T(8,128)(2,1)} %get-tuple-element.447, s32[]{:T(128)S(6)} %select_n.164), kind=kOutput, calls=%fused_computation.2.clone.1 | convolution fusion | flops 543160320 | bytes 10231812 | tf_op jit(solution)/shard_map/while/body/eval_jaxpr/qkgd,skd->kgqs/dot_general | solution.py:93
  328.4 7.2 %fusion.80 = f32[1024,1,2,128]{0,3,2,1:T(8,128)} fusion(f32[1024,1024,2]{1,0,2:T(8,128)} %get-tuple-element.407, f32[2,1024]{1,0:T(2,128)S(1)} %bitcast.126, pred[1024,1024]{0,1:T(8,128)(4,1)S(1)} %compare_and_fusion.2, f32[1024,1,2,128]{0,3,2,1:T(8,128)} %get-tuple-element.427, f32[1024,2]{0,1:T(2,128)S(1)} %get-tuple-element.408, ...), kind=kOutput, calls=%fused_computation.12.clone.1 | convolution fusion | flops 546045952 | bytes 11812873 | tf_op jit(solution)/shard_map/while/body/eval_jaxpr/kgqs,skd->qkgd/dot_general | solution.py:101
  339.0 6.3 %fusion.77 = (f32[2,1024]{1,0:T(2,128)S(1)}, f32[1024,1024,2]{1,0,2:T(8,128)}) fusion(pred[1024,1024]{0,1:T(8,128)(4,1)S(1)} %compare_and_fusion.2, bf16[1024,1,2,128]{3,0,2,1:T(8,128)(2,1)} %get-tuple-element.448, bf16[2,16384,128]{1,2,0:T(8,128)(2,1)} %get-tuple-element.447, s32[]{:T(128)S(6)} %select_n.164), kind=kOutput, calls=%fused_computation.2.clone.1 | convolution fusion | flops 543160320 | bytes 10231812 | tf_op jit(solution)/shard_map/while/body/eval_jaxpr/qkgd,skd->kgqs/dot_general | solution.py:93
  345.3 7.2 %fusion.80 = f32[1024,1,2,128]{0,3,2,1:T(8,128)} fusion(f32[1024,1024,2]{1,0,2:T(8,128)} %get-tuple-element.407, f32[2,1024]{1,0:T(2,128)S(1)} %bitcast.126, pred[1024,1024]{0,1:T(8,128)(4,1)S(1)} %compare_and_fusion.2, f32[1024,1,2,128]{0,3,2,1:T(8,128)} %get-tuple-element.427, f32[1024,2]{0,1:T(2,128)S(1)} %get-tuple-element.408, ...), kind=kOutput, calls=%fused_computation.12.clone.1 | convolution fusion | flops 546045952 | bytes 11812873 | tf_op jit(solution)/shard_map/while/body/eval_jaxpr/kgqs,skd->qkgd/dot_general | solution.py:101
  356.0 6.3 %fusion.77 = (f32[2,1024]{1,0:T(2,128)S(1)}, f32[1024,1024,2]{1,0,2:T(8,128)}) fusion(pred[1024,1024]{0,1:T(8,128)(4,1)S(1)} %compare_and_fusion.2, bf16[1024,1,2,128]{3,0,2,1:T(8,128)(2,1)} %get-tuple-element.448, bf16[2,16384,128]{1,2,0:T(8,128)(2,1)} %get-tuple-element.447, s32[]{:T(128)S(6)} %select_n.164), kind=kOutput, calls=%fused_computation.2.clone.1 | convolution fusion | flops 543160320 | bytes 10231812 | tf_op jit(solution)/shard_map/while/body/eval_jaxpr/qkgd,skd->kgqs/dot_general | solution.py:93
  362.3 7.2 %fusion.80 = f32[1024,1,2,128]{0,3,2,1:T(8,128)} fusion(f32[1024,1024,2]{1,0,2:T(8,128)} %get-tuple-element.407, f32[2,1024]{1,0:T(2,128)S(1)} %bitcast.126, pred[1024,1024]{0,1:T(8,128)(4,1)S(1)} %compare_and_fusion.2, f32[1024,1,2,128]{0,3,2,1:T(8,128)} %get-tuple-element.427, f32[1024,2]{0,1:T(2,128)S(1)} %get-tuple-element.408, ...), kind=kOutput, calls=%fused_computation.12.clone.1 | convolution fusion | flops 546045952 | bytes 11812873 | tf_op jit(solution)/shard_map/while/body/eval_jaxpr/kgqs,skd->qkgd/dot_general | solution.py:101
  372.9 6.3 %fusion.77 = (f32[2,1024]{1,0:T(2,128)S(1)}, f32[1024,1024,2]{1,0,2:T(8,128)}) fusion(pred[1024,1024]{0,1:T(8,128)(4,1)S(1)} %compare_and_fusion.2, bf16[1024,1,2,128]{3,0,2,1:T(8,128)(2,1)} %get-tuple-element.448, bf16[2,16384,128]{1,2,0:T(8,128)(2,1)} %get-tuple-element.447, s32[]{:T(128)S(6)} %select_n.164), kind=kOutput, calls=%fused_computation.2.clone.1 | convolution fusion | flops 543160320 | bytes 10231812 | tf_op jit(solution)/shard_map/while/body/eval_jaxpr/qkgd,skd->kgqs/dot_general | solution.py:93
  379.2 7.2 %fusion.80 = f32[1024,1,2,128]{0,3,2,1:T(8,128)} fusion(f32[1024,1024,2]{1,0,2:T(8,128)} %get-tuple-element.407, f32[2,1024]{1,0:T(2,128)S(1)} %bitcast.126, pred[1024,1024]{0,1:T(8,128)(4,1)S(1)} %compare_and_fusion.2, f32[1024,1,2,128]{0,3,2,1:T(8,128)} %get-tuple-element.427, f32[1024,2]{0,1:T(2,128)S(1)} %get-tuple-element.408, ...), kind=kOutput, calls=%fused_computation.12.clone.1 | convolution fusion | flops 546045952 | bytes 11812873 | tf_op jit(solution)/shard_map/while/body/eval_jaxpr/kgqs,skd->qkgd/dot_general | solution.py:101
  389.9 6.3 %fusion.77 = (f32[2,1024]{1,0:T(2,128)S(1)}, f32[1024,1024,2]{1,0,2:T(8,128)}) fusion(pred[1024,1024]{0,1:T(8,128)(4,1)S(1)} %compare_and_fusion.2, bf16[1024,1,2,128]{3,0,2,1:T(8,128)(2,1)} %get-tuple-element.448, bf16[2,16384,128]{1,2,0:T(8,128)(2,1)} %get-tuple-element.447, s32[]{:T(128)S(6)} %select_n.164), kind=kOutput, calls=%fused_computation.2.clone.1 | convolution fusion | flops 543160320 | bytes 10231812 | tf_op jit(solution)/shard_map/while/body/eval_jaxpr/qkgd,skd->kgqs/dot_general | solution.py:93
  396.2 7.2 %fusion.80 = f32[1024,1,2,128]{0,3,2,1:T(8,128)} fusion(f32[1024,1024,2]{1,0,2:T(8,128)} %get-tuple-element.407, f32[2,1024]{1,0:T(2,128)S(1)} %bitcast.126, pred[1024,1024]{0,1:T(8,128)(4,1)S(1)} %compare_and_fusion.2, f32[1024,1,2,128]{0,3,2,1:T(8,128)} %get-tuple-element.427, f32[1024,2]{0,1:T(2,128)S(1)} %get-tuple-element.408, ...), kind=kOutput, calls=%fused_computation.12.clone.1 | convolution fusion | flops 546045952 | bytes 11812873 | tf_op jit(solution)/shard_map/while/body/eval_jaxpr/kgqs,skd->qkgd/dot_general | solution.py:101
  406.8 6.3 %fusion.77 = (f32[2,1024]{1,0:T(2,128)S(1)}, f32[1024,1024,2]{1,0,2:T(8,128)}) fusion(pred[1024,1024]{0,1:T(8,128)(4,1)S(1)} %compare_and_fusion.2, bf16[1024,1,2,128]{3,0,2,1:T(8,128)(2,1)} %get-tuple-element.448, bf16[2,16384,128]{1,2,0:T(8,128)(2,1)} %get-tuple-element.447, s32[]{:T(128)S(6)} %select_n.164), kind=kOutput, calls=%fused_computation.2.clone.1 | convolution fusion | flops 543160320 | bytes 10231812 | tf_op jit(solution)/shard_map/while/body/eval_jaxpr/qkgd,skd->kgqs/dot_general | solution.py:93
  413.1 7.2 %fusion.80 = f32[1024,1,2,128]{0,3,2,1:T(8,128)} fusion(f32[1024,1024,2]{1,0,2:T(8,128)} %get-tuple-element.407, f32[2,1024]{1,0:T(2,128)S(1)} %bitcast.126, pred[1024,1024]{0,1:T(8,128)(4,1)S(1)} %compare_and_fusion.2, f32[1024,1,2,128]{0,3,2,1:T(8,128)} %get-tuple-element.427, f32[1024,2]{0,1:T(2,128)S(1)} %get-tuple-element.408, ...), kind=kOutput, calls=%fused_computation.12.clone.1 | convolution fusion | flops 546045952 | bytes 11812873 | tf_op jit(solution)/shard_map/while/body/eval_jaxpr/kgqs,skd->qkgd/dot_general | solution.py:101
  423.8 6.3 %fusion.77 = (f32[2,1024]{1,0:T(2,128)S(1)}, f32[1024,1024,2]{1,0,2:T(8,128)}) fusion(pred[1024,1024]{0,1:T(8,128)(4,1)S(1)} %compare_and_fusion.2, bf16[1024,1,2,128]{3,0,2,1:T(8,128)(2,1)} %get-tuple-element.448, bf16[2,16384,128]{1,2,0:T(8,128)(2,1)} %get-tuple-element.447, s32[]{:T(128)S(6)} %select_n.164), kind=kOutput, calls=%fused_computation.2.clone.1 | convolution fusion | flops 543160320 | bytes 10231812 | tf_op jit(solution)/shard_map/while/body/eval_jaxpr/qkgd,skd->kgqs/dot_general | solution.py:93
  430.1 7.2 %fusion.80 = f32[1024,1,2,128]{0,3,2,1:T(8,128)} fusion(f32[1024,1024,2]{1,0,2:T(8,128)} %get-tuple-element.407, f32[2,1024]{1,0:T(2,128)S(1)} %bitcast.126, pred[1024,1024]{0,1:T(8,128)(4,1)S(1)} %compare_and_fusion.2, f32[1024,1,2,128]{0,3,2,1:T(8,128)} %get-tuple-element.427, f32[1024,2]{0,1:T(2,128)S(1)} %get-tuple-element.408, ...), kind=kOutput, calls=%fused_computation.12.clone.1 | convolution fusion | flops 546045952 | bytes 11812873 | tf_op jit(solution)/shard_map/while/body/eval_jaxpr/kgqs,skd->qkgd/dot_general | solution.py:101
  440.7 6.3 %fusion.77 = (f32[2,1024]{1,0:T(2,128)S(1)}, f32[1024,1024,2]{1,0,2:T(8,128)}) fusion(pred[1024,1024]{0,1:T(8,128)(4,1)S(1)} %compare_and_fusion.2, bf16[1024,1,2,128]{3,0,2,1:T(8,128)(2,1)} %get-tuple-element.448, bf16[2,16384,128]{1,2,0:T(8,128)(2,1)} %get-tuple-element.447, s32[]{:T(128)S(6)} %select_n.164), kind=kOutput, calls=%fused_computation.2.clone.1 | convolution fusion | flops 543160320 | bytes 10231812 | tf_op jit(solution)/shard_map/while/body/eval_jaxpr/qkgd,skd->kgqs/dot_general | solution.py:93
  447.0 7.2 %fusion.80 = f32[1024,1,2,128]{0,3,2,1:T(8,128)} fusion(f32[1024,1024,2]{1,0,2:T(8,128)} %get-tuple-element.407, f32[2,1024]{1,0:T(2,128)S(1)} %bitcast.126, pred[1024,1024]{0,1:T(8,128)(4,1)S(1)} %compare_and_fusion.2, f32[1024,1,2,128]{0,3,2,1:T(8,128)} %get-tuple-element.427, f32[1024,2]{0,1:T(2,128)S(1)} %get-tuple-element.408, ...), kind=kOutput, calls=%fused_computation.12.clone.1 | convolution fusion | flops 546045952 | bytes 11812873 | tf_op jit(solution)/shard_map/while/body/eval_jaxpr/kgqs,skd->qkgd/dot_general | solution.py:101
  457.6 5.6 convolution_convert_fusion
  463.2 115.5 %reduce-scatter.2.cloned.1.call-done = bf16[128,4096]{1,0:T(8,128)(2,1)} async-done(((bf16[1024,4096]{1,0:T(8,128)(2,1)}), bf16[128,4096]{1,0:T(8,128)(2,1)}) %reduce-scatter.2.cloned.1.call-update) | async-done | bytes 1048592 | tf_op jit(solution)/shard_map/reduce_scatter | solution.py:129
  (205 shorter events, 51.4 us)
Async XLA Ops:
  6.5 451.0 %copy-start = (bf16[256,4096]{1,0:T(8,128)(2,1)S(1)}, bf16[256,4096]{1,0:T(8,128)(2,1)}, u32[]{:S(2)}) copy-start(bf16[256,4096]{1,0:T(8,128)(2,1)} %param.15) | copy-start | bytes 6291460
  6.5 116.0 %all-gather.3.cloned.1.call-start = ((), (), s32[]{:S(2)}) async-start(), calls=%async_computation.1 | async-start | bytes 9437184 | tf_op jit(solution)/shard_map/all_gather | solution.py:59
  10.7 119.7 %copy-start.3 = (bf16[4096,128]{1,0:T(8,128)(2,1)S(1)}, bf16[4096,128]{1,0:T(8,128)(2,1)}, u32[]{:S(2)}) copy-start(bf16[4096,128]{1,0:T(8,128)(2,1)} %param.14) | copy-start | bytes 3145732
  10.8 174.5 %all-gather.5.cloned.1.call-start = ((), (), s32[]{:S(2)}) async-start(), calls=%async_computation.2 | async-start | bytes 8912896 | tf_op jit(solution)/shard_map/all_gather | solution.py:114
  122.6 7.9 %copy-start.2 = (bf16[1,1024,4096]{2,1,0:T(8,128)(2,1)S(1)}, bf16[1,1024,4096]{2,1,0:T(8,128)(2,1)}, u32[]{:S(2)}) copy-start(bf16[1,1024,4096]{2,1,0:T(8,128)(2,1)} %all-gather.3.cloned.1.call-done) | copy-start | bytes 25165828
  130.5 8.1 %copy-start.5 = (s32[16]{0:T(128)S(1)}, s32[16]{0:T(128)}, u32[]{:S(2)}) copy-start(s32[16]{0:T(128)} %param.16) | copy-start | bytes 196
  134.2 444.5 %reduce-scatter.2.cloned.1.call-start = ((), (), s32[]{:S(2)}) async-start(), calls=%async_computation.3 | async-start | bytes 9437184 | tf_op jit(solution)/shard_map/reduce_scatter | solution.py:129
  139.9 45.4 %copy-start.4 = (s32[32]{0:T(128)S(1)}, s32[32]{0:T(128)}, u32[]{:S(2)}) copy-start(s32[32]{0:T(128)} %param.17) | copy-start | bytes 388
  193.0 7.0 %copy-start.1 = (f32[1024,1024,2]{1,0,2:T(8,128)S(1)}, f32[1024,1024,2]{1,0,2:T(8,128)}, u32[]{:S(2)}) copy-start(f32[1024,1024,2]{1,0,2:T(8,128)} %get-tuple-element.407) | copy-start | bytes 25165828 | tf_op jit(solution)/shard_map/while
  209.7 7.2 %copy-start.1 = (f32[1024,1024,2]{1,0,2:T(8,128)S(1)}, f32[1024,1024,2]{1,0,2:T(8,128)}, u32[]{:S(2)}) copy-start(f32[1024,1024,2]{1,0,2:T(8,128)} %get-tuple-element.407) | copy-start | bytes 25165828 | tf_op jit(solution)/shard_map/while
  226.7 7.2 %copy-start.1 = (f32[1024,1024,2]{1,0,2:T(8,128)S(1)}, f32[1024,1024,2]{1,0,2:T(8,128)}, u32[]{:S(2)}) copy-start(f32[1024,1024,2]{1,0,2:T(8,128)} %get-tuple-element.407) | copy-start | bytes 25165828 | tf_op jit(solution)/shard_map/while
  243.6 7.2 %copy-start.1 = (f32[1024,1024,2]{1,0,2:T(8,128)S(1)}, f32[1024,1024,2]{1,0,2:T(8,128)}, u32[]{:S(2)}) copy-start(f32[1024,1024,2]{1,0,2:T(8,128)} %get-tuple-element.407) | copy-start | bytes 25165828 | tf_op jit(solution)/shard_map/while
  260.6 7.2 %copy-start.1 = (f32[1024,1024,2]{1,0,2:T(8,128)S(1)}, f32[1024,1024,2]{1,0,2:T(8,128)}, u32[]{:S(2)}) copy-start(f32[1024,1024,2]{1,0,2:T(8,128)} %get-tuple-element.407) | copy-start | bytes 25165828 | tf_op jit(solution)/shard_map/while
  277.5 7.2 %copy-start.1 = (f32[1024,1024,2]{1,0,2:T(8,128)S(1)}, f32[1024,1024,2]{1,0,2:T(8,128)}, u32[]{:S(2)}) copy-start(f32[1024,1024,2]{1,0,2:T(8,128)} %get-tuple-element.407) | copy-start | bytes 25165828 | tf_op jit(solution)/shard_map/while
  294.5 7.2 %copy-start.1 = (f32[1024,1024,2]{1,0,2:T(8,128)S(1)}, f32[1024,1024,2]{1,0,2:T(8,128)}, u32[]{:S(2)}) copy-start(f32[1024,1024,2]{1,0,2:T(8,128)} %get-tuple-element.407) | copy-start | bytes 25165828 | tf_op jit(solution)/shard_map/while
  311.4 7.2 %copy-start.1 = (f32[1024,1024,2]{1,0,2:T(8,128)S(1)}, f32[1024,1024,2]{1,0,2:T(8,128)}, u32[]{:S(2)}) copy-start(f32[1024,1024,2]{1,0,2:T(8,128)} %get-tuple-element.407) | copy-start | bytes 25165828 | tf_op jit(solution)/shard_map/while
  328.4 7.2 %copy-start.1 = (f32[1024,1024,2]{1,0,2:T(8,128)S(1)}, f32[1024,1024,2]{1,0,2:T(8,128)}, u32[]{:S(2)}) copy-start(f32[1024,1024,2]{1,0,2:T(8,128)} %get-tuple-element.407) | copy-start | bytes 25165828 | tf_op jit(solution)/shard_map/while
  345.3 7.2 %copy-start.1 = (f32[1024,1024,2]{1,0,2:T(8,128)S(1)}, f32[1024,1024,2]{1,0,2:T(8,128)}, u32[]{:S(2)}) copy-start(f32[1024,1024,2]{1,0,2:T(8,128)} %get-tuple-element.407) | copy-start | bytes 25165828 | tf_op jit(solution)/shard_map/while
  362.3 7.2 %copy-start.1 = (f32[1024,1024,2]{1,0,2:T(8,128)S(1)}, f32[1024,1024,2]{1,0,2:T(8,128)}, u32[]{:S(2)}) copy-start(f32[1024,1024,2]{1,0,2:T(8,128)} %get-tuple-element.407) | copy-start | bytes 25165828 | tf_op jit(solution)/shard_map/while
  379.2 7.2 %copy-start.1 = (f32[1024,1024,2]{1,0,2:T(8,128)S(1)}, f32[1024,1024,2]{1,0,2:T(8,128)}, u32[]{:S(2)}) copy-start(f32[1024,1024,2]{1,0,2:T(8,128)} %get-tuple-element.407) | copy-start | bytes 25165828 | tf_op jit(solution)/shard_map/while
  396.2 7.2 %copy-start.1 = (f32[1024,1024,2]{1,0,2:T(8,128)S(1)}, f32[1024,1024,2]{1,0,2:T(8,128)}, u32[]{:S(2)}) copy-start(f32[1024,1024,2]{1,0,2:T(8,128)} %get-tuple-element.407) | copy-start | bytes 25165828 | tf_op jit(solution)/shard_map/while
  413.1 7.2 %copy-start.1 = (f32[1024,1024,2]{1,0,2:T(8,128)S(1)}, f32[1024,1024,2]{1,0,2:T(8,128)}, u32[]{:S(2)}) copy-start(f32[1024,1024,2]{1,0,2:T(8,128)} %get-tuple-element.407) | copy-start | bytes 25165828 | tf_op jit(solution)/shard_map/while
  430.1 7.2 %copy-start.1 = (f32[1024,1024,2]{1,0,2:T(8,128)S(1)}, f32[1024,1024,2]{1,0,2:T(8,128)}, u32[]{:S(2)}) copy-start(f32[1024,1024,2]{1,0,2:T(8,128)} %get-tuple-element.407) | copy-start | bytes 25165828 | tf_op jit(solution)/shard_map/while
  447.0 7.2 %copy-start.1 = (f32[1024,1024,2]{1,0,2:T(8,128)S(1)}, f32[1024,1024,2]{1,0,2:T(8,128)}, u32[]{:S(2)}) copy-start(f32[1024,1024,2]{1,0,2:T(8,128)} %get-tuple-element.407) | copy-start | bytes 25165828 | tf_op jit(solution)/shard_map/while
Sparse Core Ops, SparseCore 0:
  10.9 111.6 all-gather.2
  134.4 50.9 all-gather.4
  463.3 115.3 reduce-scatter.1
where the time goes:
time: 586 us; the launch traced here: 585 us
  waiting for transfers between devices  264 us (45%)
  matrix products  237 us (40%)
  other arithmetic  64.2 us (11%)
  between operations  13.3 us (2%)
    reduce_scatter x1, waiting for transfers between devices, per_device(): lax.psum_scatter(jnp.dot(attended, o_weight, preferred_element_type=jnp.f...  115 us
    dot_general x16, matrix products, attend(): jnp.einsum('kgqs,skd->qkgd', weights.astype(jnp.bfloat16), value_rows, pr...  115 us
    all_gather x1, waiting for transfers between devices, per_device(): portion = lax.all_gather(normed, 'tensor', axis=1, tiled=True)  111 us
    dot_general x16, matrix products, attend(): jnp.einsum('qkgd,skd->kgqs', queries, key_rows, preferred_element_type=jn...  100 us
    all_gather x1, waiting for transfers between devices, per_device(): gathered = lax.all_gather(kv_pair, 'context', axis=1, tiled=True)  37.5 us
    reduce_sum x16, other arithmetic, attend(): row_sum = row_sum * factor + jnp.sum(weights, axis=-1)  31.5 us
    and x16, other arithmetic, attend(): (key_places[None, :] <= query_places[:, None]) & (key_docs[None, :] == qu...  19.1 us
  transfers between devices with their start and end apart: 3, of which 3 were waited for; matrix products, arithmetic and copies ran while one was open for 2% of the time, Pallas kernels for 0%

commit v1 on v0

--- a/solution.py
+++ b/solution.py
@@ -1,13 +1,24 @@
+import functools
 import math
 import jax
 import jax.numpy as jnp
 from jax import lax
 from jax.sharding import PartitionSpec as P
+from jax.lax import all_to_all, axis_size
 
 HEAD_DIM = 128
 rope_theta = 500000.0
 epsilon = 1e-05
 masked_score = -1e30
+
+
+def _finish_sample(z_in, shard_axis):
+    new = jnp.stack(axis_size(shard_axis) * [z_in], 0)
+    y_new = all_to_all(new, axis_name=shard_axis, split_axis=0, concat_axis=0)
+    return jnp.concatenate(y_new, 1)
+
+
+shape_the_stages_all = functools.partial(_finish_sample, shard_axis="context")
 
 
 def positions(rows, span_order, span_rows):
@@ -111,7 +122,7 @@
         jnp.zeros((kv_local, group_size, tok_dev), jnp.float32),
         jnp.zeros((tok_dev, kv_local, group_size, head_dim), jnp.float32),
     )
-    gathered = lax.all_gather(kv_pair, "context", axis=1, tiled=True)
+    gathered = shape_the_stages_all(kv_pair)
 
     def visit_block(block_index, carried):
         offset = block_index * tok_dev

time: 586 us -> 641 us (1.094)
  waiting for transfers between devices: 264 us -> 304 us
  local copies, waits for them, and re-layouts: 5.24 us -> 18.1 us
    all_to_all x0 -> x1, waiting for transfers between devices: none -> 81.5 us  [_finish_sample(): y_new = all_to_all(new, axis_name=shard_axis, split_axis=0, concat_axis=0)]
    all_gather x1 -> x0, waiting for transfers between devices: 37.5 us -> none  [per_device(): gathered = lax.all_gather(kv_pair, 'context', axis=1, tiled=True)]
    all_to_all x0 -> x1, local copies, waits for them, and re-layouts: none -> 7.51 us  [_finish_sample(): y_new = all_to_all(new, axis_name=shard_axis, split_axis=0, concat_axis=0)]
where the time goes in v1:
time: 641 us; the launch traced here: 640 us
  waiting for transfers between devices  304 us (47%)
  matrix products  233 us (36%)
  other arithmetic  63.5 us (10%)
  local copies, waits for them, and re-layouts  18.1 us (3%)
  between operations  13.6 us (2%)
    dot_general x16, matrix products, attend(): jnp.einsum('kgqs,skd->qkgd', weights.astype(jnp.bfloat16), value_rows, pr...  114 us
    reduce_scatter x1, waiting for transfers between devices, per_device(): lax.psum_scatter(jnp.dot(attended, o_weight, preferred_element_type=jnp.f...  112 us
    all_gather x1, waiting for transfers between devices, per_device(): portion = lax.all_gather(normed, 'tensor', axis=1, tiled=True)  111 us
    dot_general x16, matrix products, attend(): jnp.einsum('qkgd,skd->kgqs', queries, key_rows, preferred_element_type=jn...  98 us
    all_to_all x1, waiting for transfers between devices, _finish_sample(): y_new = all_to_all(new, axis_name=shard_axis, split_axis=0, concat_axis=0)  81.5 us
    reduce_sum x16, other arithmetic, attend(): row_sum = row_sum * factor + jnp.sum(weights, axis=-1)  31.5 us
    and x16, other arithmetic, attend(): (key_places[None, :] <= query_places[:, None]) & (key_docs[None, :] == qu...  19.1 us
  transfers between devices with their start and end apart: 3, of which 3 were waited for; matrix products, arithmetic and copies ran while one was open for 2% of the time, Pallas kernels for 0%

profile of v1, /device:TPU:1, one launch (start us, length us, event | category | flops | bytes accessed | tf_op | source)
XLA Modules:
  0.0 640.0 jit_solution(6209834441240537270)
XLA Ops:
  8.2 2.5 fusion.36
  11.7 110.9 %all-gather.2.cloned.1.call-done = bf16[1,1024,4096]{2,1,0:T(8,128)(2,1)} async-done(((bf16[1,128,4096]{2,1,0:T(8,128)(2,1)}), bf16[1,1024,4096]{2,1,0:T(8,128)(2,1)}) %all-gather.2.cloned.1.call-update) | async-done | bytes 8388624 | tf_op jit(solution)/shard_map/all_gather | solution.py:70
  122.6 6.7 %fusion.37 = f32[1024,1,128]{0,2,1:T(8,128)S(1)} fusion(bf16[4096,128]{1,0:T(8,128)(2,1)} %param.13, bf16[1,1024,4096]{2,1,0:T(8,128)(2,1)} %all-gather.2.cloned.1.call-done), kind=kOutput, calls=%fused_computation.56 | convolution fusion | flops 1073741824 | bytes 9961472 | tf_op jit(solution)/shard_map/dot_general | solution.py:77
  130.5 2.9 fusion.43
  133.7 5.1 stack.8
  138.8 5.7 all-to-all-start
  144.8 4.1 copy.38
  150.2 6.3 fusion.28
  157.8 81.5 %all-to-all-done = bf16[16,2,1024,128]{3,2,1,0:T(8,128)(2,1)} async-done(((bf16[16,2,1024,128]{3,2,1,0:T(8,128)(2,1)}), bf16[16,2,1024,128]{3,2,1,0:T(8,128)(2,1)}, u32[]{:S(2)}, u32[]{:S(2)}) %all-to-all-start) | async-done | bytes 8388640 | tf_op jit(solution)/shard_map/all_to_all | solution.py:17
  239.3 7.5 %copy.32 = bf16[16,2,1024,128]{3,2,0,1:T(8,128)(2,1)} copy(bf16[16,2,1024,128]{3,2,1,0:T(8,128)(2,1)} %all-to-all-done) | data formatting | bytes 16777216 | tf_op jit(solution)/shard_map/all_to_all | solution.py:17
  246.8 267.6 %while.20 = (s32[]{:T(128)}, f32[1,2,1024]{2,1,0:T(2,128)S(1)}, f32[1,2,1024]{2,1,0:T(2,128)S(1)}, f32[1024,1,2,128]{0,3,2,1:T(8,128)}, s32[32]{0:T(128)S(1)}, /...) while((s32[]{:T(128)}, f32[1,2,1024]{2,1,0:T(2,128)S(1)}, ...), condition=%wide.region_9.10_spmd.clone, body=%wide.region_4.9_spmd.clone.sunk | while | flops 1100931072 | bytes 66236864 | solution.py:132
  248.2 6.1 fusion.77
  254.4 6.9 %fusion.80 = f32[1024,1,2,128]{0,3,2,1:T(8,128)} fusion(f32[1024,1024,2]{1,0,2:T(8,128)} %get-tuple-element.427, f32[2,1024]{1,0:T(2,128)S(1)} %bitcast.128, pred[1024,1024]{0,1:T(8,128)(4,1)S(1)} %compare_and_fusion.2, f32[1024,1,2,128]{0,3,2,1:T(8,128)} %get-tuple-element.447, f32[1024,2]{0,1:T(2,128)S(1)} %get-tuple-element.428, ...), kind=kOutput, calls=%fused_computation.12.clone.1 | convolution fusion | flops 546045952 | bytes 11812873 | tf_op jit(solution)/shard_map/while/body/eval_jaxpr/kgqs,skd->qkgd/dot_general | solution.py:112
  261.3 2.0 fusion.79
  264.7 6.1 fusion.77
  270.9 7.1 %fusion.80 = f32[1024,1,2,128]{0,3,2,1:T(8,128)} fusion(f32[1024,1024,2]{1,0,2:T(8,128)} %get-tuple-element.427, f32[2,1024]{1,0:T(2,128)S(1)} %bitcast.128, pred[1024,1024]{0,1:T(8,128)(4,1)S(1)} %compare_and_fusion.2, f32[1024,1,2,128]{0,3,2,1:T(8,128)} %get-tuple-element.447, f32[1024,2]{0,1:T(2,128)S(1)} %get-tuple-element.428, ...), kind=kOutput, calls=%fused_computation.12.clone.1 | convolution fusion | flops 546045952 | bytes 11812873 | tf_op jit(solution)/shard_map/while/body/eval_jaxpr/kgqs,skd->qkgd/dot_general | solution.py:112
  278.0 2.0 fusion.79
  281.5 6.1 fusion.77
  287.6 7.1 %fusion.80 = f32[1024,1,2,128]{0,3,2,1:T(8,128)} fusion(f32[1024,1024,2]{1,0,2:T(8,128)} %get-tuple-element.427, f32[2,1024]{1,0:T(2,128)S(1)} %bitcast.128, pred[1024,1024]{0,1:T(8,128)(4,1)S(1)} %compare_and_fusion.2, f32[1024,1,2,128]{0,3,2,1:T(8,128)} %get-tuple-element.447, f32[1024,2]{0,1:T(2,128)S(1)} %get-tuple-element.428, ...), kind=kOutput, calls=%fused_computation.12.clone.1 | convolution fusion | flops 546045952 | bytes 11812873 | tf_op jit(solution)/shard_map/while/body/eval_jaxpr/kgqs,skd->qkgd/dot_general | solution.py:112
  298.2 6.1 fusion.77
  304.4 7.1 %fusion.80 = f32[1024,1,2,128]{0,3,2,1:T(8,128)} fusion(f32[1024,1024,2]{1,0,2:T(8,128)} %get-tuple-element.427, f32[2,1024]{1,0:T(2,128)S(1)} %bitcast.128, pred[1024,1024]{0,1:T(8,128)(4,1)S(1)} %compare_and_fusion.2, f32[1024,1,2,128]{0,3,2,1:T(8,128)} %get-tuple-element.447, f32[1024,2]{0,1:T(2,128)S(1)} %get-tuple-element.428, ...), kind=kOutput, calls=%fused_computation.12.clone.1 | convolution fusion | flops 546045952 | bytes 11812873 | tf_op jit(solution)/shard_map/while/body/eval_jaxpr/kgqs,skd->qkgd/dot_general | solution.py:112
  311.5 2.0 fusion.79
  314.9 6.1 fusion.77
  321.1 7.1 %fusion.80 = f32[1024,1,2,128]{0,3,2,1:T(8,128)} fusion(f32[1024,1024,2]{1,0,2:T(8,128)} %get-tuple-element.427, f32[2,1024]{1,0:T(2,128)S(1)} %bitcast.128, pred[1024,1024]{0,1:T(8,128)(4,1)S(1)} %compare_and_fusion.2, f32[1024,1,2,128]{0,3,2,1:T(8,128)} %get-tuple-element.447, f32[1024,2]{0,1:T(2,128)S(1)} %get-tuple-element.428, ...), kind=kOutput, calls=%fused_computation.12.clone.1 | convolution fusion | flops 546045952 | bytes 11812873 | tf_op jit(solution)/shard_map/while/body/eval_jaxpr/kgqs,skd->qkgd/dot_general | solution.py:112
  331.7 6.1 fusion.77
  337.8 7.1 %fusion.80 = f32[1024,1,2,128]{0,3,2,1:T(8,128)} fusion(f32[1024,1024,2]{1,0,2:T(8,128)} %get-tuple-element.427, f32[2,1024]{1,0:T(2,128)S(1)} %bitcast.128, pred[1024,1024]{0,1:T(8,128)(4,1)S(1)} %compare_and_fusion.2, f32[1024,1,2,128]{0,3,2,1:T(8,128)} %get-tuple-element.447, f32[1024,2]{0,1:T(2,128)S(1)} %get-tuple-element.428, ...), kind=kOutput, calls=%fused_computation.12.clone.1 | convolution fusion | flops 546045952 | bytes 11812873 | tf_op jit(solution)/shard_map/while/body/eval_jaxpr/kgqs,skd->qkgd/dot_general | solution.py:112
  348.4 6.1 fusion.77
  354.6 7.1 %fusion.80 = f32[1024,1,2,128]{0,3,2,1:T(8,128)} fusion(f32[1024,1024,2]{1,0,2:T(8,128)} %get-tuple-element.427, f32[2,1024]{1,0:T(2,128)S(1)} %bitcast.128, pred[1024,1024]{0,1:T(8,128)(4,1)S(1)} %compare_and_fusion.2, f32[1024,1,2,128]{0,3,2,1:T(8,128)} %get-tuple-element.447, f32[1024,2]{0,1:T(2,128)S(1)} %get-tuple-element.428, ...), kind=kOutput, calls=%fused_computation.12.clone.1 | convolution fusion | flops 546045952 | bytes 11812873 | tf_op jit(solution)/shard_map/while/body/eval_jaxpr/kgqs,skd->qkgd/dot_general | solution.py:112
  365.2 6.1 fusion.77
  371.3 7.1 %fusion.80 = f32[1024,1,2,128]{0,3,2,1:T(8,128)} fusion(f32[1024,1024,2]{1,0,2:T(8,128)} %get-tuple-element.427, f32[2,1024]{1,0:T(2,128)S(1)} %bitcast.128, pred[1024,1024]{0,1:T(8,128)(4,1)S(1)} %compare_and_fusion.2, f32[1024,1,2,128]{0,3,2,1:T(8,128)} %get-tuple-element.447, f32[1024,2]{0,1:T(2,128)S(1)} %get-tuple-element.428, ...), kind=kOutput, calls=%fused_computation.12.clone.1 | convolution fusion | flops 546045952 | bytes 11812873 | tf_op jit(solution)/shard_map/while/body/eval_jaxpr/kgqs,skd->qkgd/dot_general | solution.py:112
  381.9 6.1 fusion.77
  388.1 7.1 %fusion.80 = f32[1024,1,2,128]{0,3,2,1:T(8,128)} fusion(f32[1024,1024,2]{1,0,2:T(8,128)} %get-tuple-element.427, f32[2,1024]{1,0:T(2,128)S(1)} %bitcast.128, pred[1024,1024]{0,1:T(8,128)(4,1)S(1)} %compare_and_fusion.2, f32[1024,1,2,128]{0,3,2,1:T(8,128)} %get-tuple-element.447, f32[1024,2]{0,1:T(2,128)S(1)} %get-tuple-element.428, ...), kind=kOutput, calls=%fused_computation.12.clone.1 | convolution fusion | flops 546045952 | bytes 11812873 | tf_op jit(solution)/shard_map/while/body/eval_jaxpr/kgqs,skd->qkgd/dot_general | solution.py:112
  398.6 6.1 fusion.77
  404.8 7.1 %fusion.80 = f32[1024,1,2,128]{0,3,2,1:T(8,128)} fusion(f32[1024,1024,2]{1,0,2:T(8,128)} %get-tuple-element.427, f32[2,1024]{1,0:T(2,128)S(1)} %bitcast.128, pred[1024,1024]{0,1:T(8,128)(4,1)S(1)} %compare_and_fusion.2, f32[1024,1,2,128]{0,3,2,1:T(8,128)} %get-tuple-element.447, f32[1024,2]{0,1:T(2,128)S(1)} %get-tuple-element.428, ...), kind=kOutput, calls=%fused_computation.12.clone.1 | convolution fusion | flops 546045952 | bytes 11812873 | tf_op jit(solution)/shard_map/while/body/eval_jaxpr/kgqs,skd->qkgd/dot_general | solution.py:112
  415.4 6.1 fusion.77
  421.5 7.1 %fusion.80 = f32[1024,1,2,128]{0,3,2,1:T(8,128)} fusion(f32[1024,1024,2]{1,0,2:T(8,128)} %get-tuple-element.427, f32[2,1024]{1,0:T(2,128)S(1)} %bitcast.128, pred[1024,1024]{0,1:T(8,128)(4,1)S(1)} %compare_and_fusion.2, f32[1024,1,2,128]{0,3,2,1:T(8,128)} %get-tuple-element.447, f32[1024,2]{0,1:T(2,128)S(1)} %get-tuple-element.428, ...), kind=kOutput, calls=%fused_computation.12.clone.1 | convolution fusion | flops 546045952 | bytes 11812873 | tf_op jit(solution)/shard_map/while/body/eval_jaxpr/kgqs,skd->qkgd/dot_general | solution.py:112
  432.1 6.1 fusion.77
  438.3 7.1 %fusion.80 = f32[1024,1,2,128]{0,3,2,1:T(8,128)} fusion(f32[1024,1024,2]{1,0,2:T(8,128)} %get-tuple-element.427, f32[2,1024]{1,0:T(2,128)S(1)} %bitcast.128, pred[1024,1024]{0,1:T(8,128)(4,1)S(1)} %compare_and_fusion.2, f32[1024,1,2,128]{0,3,2,1:T(8,128)} %get-tuple-element.447, f32[1024,2]{0,1:T(2,128)S(1)} %get-tuple-element.428, ...), kind=kOutput, calls=%fused_computation.12.clone.1 | convolution fusion | flops 546045952 | bytes 11812873 | tf_op jit(solution)/shard_map/while/body/eval_jaxpr/kgqs,skd->qkgd/dot_general | solution.py:112
  448.9 6.1 fusion.77
  455.0 7.1 %fusion.80 = f32[1024,1,2,128]{0,3,2,1:T(8,128)} fusion(f32[1024,1024,2]{1,0,2:T(8,128)} %get-tuple-element.427, f32[2,1024]{1,0:T(2,128)S(1)} %bitcast.128, pred[1024,1024]{0,1:T(8,128)(4,1)S(1)} %compare_and_fusion.2, f32[1024,1,2,128]{0,3,2,1:T(8,128)} %get-tuple-element.447, f32[1024,2]{0,1:T(2,128)S(1)} %get-tuple-element.428, ...), kind=kOutput, calls=%fused_computation.12.clone.1 | convolution fusion | flops 546045952 | bytes 11812873 | tf_op jit(solution)/shard_map/while/body/eval_jaxpr/kgqs,skd->qkgd/dot_general | solution.py:112
  465.6 6.1 fusion.77
  471.8 7.1 %fusion.80 = f32[1024,1,2,128]{0,3,2,1:T(8,128)} fusion(f32[1024,1024,2]{1,0,2:T(8,128)} %get-tuple-element.427, f32[2,1024]{1,0:T(2,128)S(1)} %bitcast.128, pred[1024,1024]{0,1:T(8,128)(4,1)S(1)} %compare_and_fusion.2, f32[1024,1,2,128]{0,3,2,1:T(8,128)} %get-tuple-element.447, f32[1024,2]{0,1:T(2,128)S(1)} %get-tuple-element.428, ...), kind=kOutput, calls=%fused_computation.12.clone.1 | convolution fusion | flops 546045952 | bytes 11812873 | tf_op jit(solution)/shard_map/while/body/eval_jaxpr/kgqs,skd->qkgd/dot_general | solution.py:112
  482.4 6.1 fusion.77
  488.5 7.1 %fusion.80 = f32[1024,1,2,128]{0,3,2,1:T(8,128)} fusion(f32[1024,1024,2]{1,0,2:T(8,128)} %get-tuple-element.427, f32[2,1024]{1,0:T(2,128)S(1)} %bitcast.128, pred[1024,1024]{0,1:T(8,128)(4,1)S(1)} %compare_and_fusion.2, f32[1024,1,2,128]{0,3,2,1:T(8,128)} %get-tuple-element.447, f32[1024,2]{0,1:T(2,128)S(1)} %get-tuple-element.428, ...), kind=kOutput, calls=%fused_computation.12.clone.1 | convolution fusion | flops 546045952 | bytes 11812873 | tf_op jit(solution)/shard_map/while/body/eval_jaxpr/kgqs,skd->qkgd/dot_general | solution.py:112
  499.1 6.1 fusion.77
  505.2 7.1 %fusion.80 = f32[1024,1,2,128]{0,3,2,1:T(8,128)} fusion(f32[1024,1024,2]{1,0,2:T(8,128)} %get-tuple-element.427, f32[2,1024]{1,0:T(2,128)S(1)} %bitcast.128, pred[1024,1024]{0,1:T(8,128)(4,1)S(1)} %compare_and_fusion.2, f32[1024,1,2,128]{0,3,2,1:T(8,128)} %get-tuple-element.447, f32[1024,2]{0,1:T(2,128)S(1)} %get-tuple-element.428, ...), kind=kOutput, calls=%fused_computation.12.clone.1 | convolution fusion | flops 546045952 | bytes 11812873 | tf_op jit(solution)/shard_map/while/body/eval_jaxpr/kgqs,skd->qkgd/dot_general | solution.py:112
  515.7 5.6 convolution_convert_fusion
  521.4 111.8 %reduce-scatter.2.cloned.1.call-done = bf16[128,4096]{1,0:T(8,128)(2,1)} async-done(((bf16[1024,4096]{1,0:T(8,128)(2,1)}), bf16[128,4096]{1,0:T(8,128)(2,1)}) %reduce-scatter.2.cloned.1.call-update) | async-done | bytes 1048592 | tf_op jit(solution)/shard_map/reduce_scatter | solution.py:140
  (207 shorter events, 56.7 us)
Async XLA Ops:
  6.5 509.2 %copy-start = (bf16[256,4096]{1,0:T(8,128)(2,1)S(1)}, bf16[256,4096]{1,0:T(8,128)(2,1)}, u32[]{:S(2)}) copy-start(bf16[256,4096]{1,0:T(8,128)(2,1)} %param.15) | copy-start | bytes 6291460
  6.5 116.0 %all-gather.2.cloned.1.call-start = ((), (), s32[]{:S(2)}) async-start(), calls=%async_computation.2 | async-start | bytes 9437184 | tf_op jit(solution)/shard_map/all_gather | solution.py:70
  10.7 119.7 %copy-start.3 = (bf16[4096,128]{1,0:T(8,128)(2,1)S(1)}, bf16[4096,128]{1,0:T(8,128)(2,1)}, u32[]{:S(2)}) copy-start(bf16[4096,128]{1,0:T(8,128)(2,1)} %param.14) | copy-start | bytes 3145732
  122.6 7.9 %copy-start.2 = (bf16[1,1024,4096]{2,1,0:T(8,128)(2,1)S(1)}, bf16[1,1024,4096]{2,1,0:T(8,128)(2,1)}, u32[]{:S(2)}) copy-start(bf16[1,1024,4096]{2,1,0:T(8,128)(2,1)} %all-gather.2.cloned.1.call-done) | copy-start | bytes 25165828
  138.8 10.1 %copy-start.5 = (s32[16]{0:T(128)S(1)}, s32[16]{0:T(128)}, u32[]{:S(2)}) copy-start(s32[16]{0:T(128)} %param.16) | copy-start | bytes 196
  138.8 100.4 %all-to-all-start = ((bf16[16,2,1024,128]{3,2,1,0:T(8,128)(2,1)}), bf16[16,2,1024,128]{3,2,1,0:T(8,128)(2,1)}, u32[]{:S(2)}, u32[]{:S(2)}) async-start(bf16[16,2,1024,128]{3,2,1,0:T(8,128)(2,1)} %stack.8), calls=%async_computation | async-start | bytes 16777216 | tf_op jit(solution)/shard_map/all_to_all | solution.py:17
  144.6 488.6 %reduce-scatter.2.cloned.1.call-start = ((), (), s32[]{:S(2)}) async-start(), calls=%async_computation.3 | async-start | bytes 9437184 | tf_op jit(solution)/shard_map/reduce_scatter | solution.py:140
  157.8 89.0 %copy-start.4 = (s32[32]{0:T(128)S(1)}, s32[32]{0:T(128)}, u32[]{:S(2)}) copy-start(s32[32]{0:T(128)} %param.17) | copy-start | bytes 388
  254.3 6.9 %copy-start.1 = (f32[1024,1024,2]{1,0,2:T(8,128)S(1)}, f32[1024,1024,2]{1,0,2:T(8,128)}, u32[]{:S(2)}) copy-start(f32[1024,1024,2]{1,0,2:T(8,128)} %get-tuple-element.427) | copy-start | bytes 25165828 | tf_op jit(solution)/shard_map/while
  270.9 7.1 %copy-start.1 = (f32[1024,1024,2]{1,0,2:T(8,128)S(1)}, f32[1024,1024,2]{1,0,2:T(8,128)}, u32[]{:S(2)}) copy-start(f32[1024,1024,2]{1,0,2:T(8,128)} %get-tuple-element.427) | copy-start | bytes 25165828 | tf_op jit(solution)/shard_map/while
  287.6 7.1 %copy-start.1 = (f32[1024,1024,2]{1,0,2:T(8,128)S(1)}, f32[1024,1024,2]{1,0,2:T(8,128)}, u32[]{:S(2)}) copy-start(f32[1024,1024,2]{1,0,2:T(8,128)} %get-tuple-element.427) | copy-start | bytes 25165828 | tf_op jit(solution)/shard_map/while
  304.3 7.1 %copy-start.1 = (f32[1024,1024,2]{1,0,2:T(8,128)S(1)}, f32[1024,1024,2]{1,0,2:T(8,128)}, u32[]{:S(2)}) copy-start(f32[1024,1024,2]{1,0,2:T(8,128)} %get-tuple-element.427) | copy-start | bytes 25165828 | tf_op jit(solution)/shard_map/while
  321.1 7.1 %copy-start.1 = (f32[1024,1024,2]{1,0,2:T(8,128)S(1)}, f32[1024,1024,2]{1,0,2:T(8,128)}, u32[]{:S(2)}) copy-start(f32[1024,1024,2]{1,0,2:T(8,128)} %get-tuple-element.427) | copy-start | bytes 25165828 | tf_op jit(solution)/shard_map/while
  337.8 7.1 %copy-start.1 = (f32[1024,1024,2]{1,0,2:T(8,128)S(1)}, f32[1024,1024,2]{1,0,2:T(8,128)}, u32[]{:S(2)}) copy-start(f32[1024,1024,2]{1,0,2:T(8,128)} %get-tuple-element.427) | copy-start | bytes 25165828 | tf_op jit(solution)/shard_map/while
  354.6 7.1 %copy-start.1 = (f32[1024,1024,2]{1,0,2:T(8,128)S(1)}, f32[1024,1024,2]{1,0,2:T(8,128)}, u32[]{:S(2)}) copy-start(f32[1024,1024,2]{1,0,2:T(8,128)} %get-tuple-element.427) | copy-start | bytes 25165828 | tf_op jit(solution)/shard_map/while
  371.3 7.1 %copy-start.1 = (f32[1024,1024,2]{1,0,2:T(8,128)S(1)}, f32[1024,1024,2]{1,0,2:T(8,128)}, u32[]{:S(2)}) copy-start(f32[1024,1024,2]{1,0,2:T(8,128)} %get-tuple-element.427) | copy-start | bytes 25165828 | tf_op jit(solution)/shard_map/while
  388.0 7.1 %copy-start.1 = (f32[1024,1024,2]{1,0,2:T(8,128)S(1)}, f32[1024,1024,2]{1,0,2:T(8,128)}, u32[]{:S(2)}) copy-start(f32[1024,1024,2]{1,0,2:T(8,128)} %get-tuple-element.427) | copy-start | bytes 25165828 | tf_op jit(solution)/shard_map/while
  404.8 7.1 %copy-start.1 = (f32[1024,1024,2]{1,0,2:T(8,128)S(1)}, f32[1024,1024,2]{1,0,2:T(8,128)}, u32[]{:S(2)}) copy-start(f32[1024,1024,2]{1,0,2:T(8,128)} %get-tuple-element.427) | copy-start | bytes 25165828 | tf_op jit(solution)/shard_map/while
  421.5 7.1 %copy-start.1 = (f32[1024,1024,2]{1,0,2:T(8,128)S(1)}, f32[1024,1024,2]{1,0,2:T(8,128)}, u32[]{:S(2)}) copy-start(f32[1024,1024,2]{1,0,2:T(8,128)} %get-tuple-element.427) | copy-start | bytes 25165828 | tf_op jit(solution)/shard_map/while
  438.3 7.1 %copy-start.1 = (f32[1024,1024,2]{1,0,2:T(8,128)S(1)}, f32[1024,1024,2]{1,0,2:T(8,128)}, u32[]{:S(2)}) copy-start(f32[1024,1024,2]{1,0,2:T(8,128)} %get-tuple-element.427) | copy-start | bytes 25165828 | tf_op jit(solution)/shard_map/while
  455.0 7.1 %copy-start.1 = (f32[1024,1024,2]{1,0,2:T(8,128)S(1)}, f32[1024,1024,2]{1,0,2:T(8,128)}, u32[]{:S(2)}) copy-start(f32[1024,1024,2]{1,0,2:T(8,128)} %get-tuple-element.427) | copy-start | bytes 25165828 | tf_op jit(solution)/shard_map/while
  471.8 7.1 %copy-start.1 = (f32[1024,1024,2]{1,0,2:T(8,128)S(1)}, f32[1024,1024,2]{1,0,2:T(8,128)}, u32[]{:S(2)}) copy-start(f32[1024,1024,2]{1,0,2:T(8,128)} %get-tuple-element.427) | copy-start | bytes 25165828 | tf_op jit(solution)/shard_map/while
  488.5 7.1 %copy-start.1 = (f32[1024,1024,2]{1,0,2:T(8,128)S(1)}, f32[1024,1024,2]{1,0,2:T(8,128)}, u32[]{:S(2)}) copy-start(f32[1024,1024,2]{1,0,2:T(8,128)} %get-tuple-element.427) | copy-start | bytes 25165828 | tf_op jit(solution)/shard_map/while
  505.2 7.1 %copy-start.1 = (f32[1024,1024,2]{1,0,2:T(8,128)S(1)}, f32[1024,1024,2]{1,0,2:T(8,128)}, u32[]{:S(2)}) copy-start(f32[1024,1024,2]{1,0,2:T(8,128)} %get-tuple-element.427) | copy-start | bytes 25165828 | tf_op jit(solution)/shard_map/while
Sparse Core Ops, SparseCore 0:
  10.9 111.6 all-gather.1
  521.5 111.6 reduce-scatter.1
